TPU v7x, 32 devices: a whole 2x2x4 slice. The times are simulated.
32 devices in a mesh: grp: 4 (over z), row: 8 (over y, x, core).
Axes of the slice: x: 2, y: 2, z: 4, core: 2. Of those that a mesh axis runs over, the one named last changes fastest.
Arguments:
- basis: float32 [8192, 1024], P(('grp', 'row')), may hold values from -40 to 40
- block: float32 [8192, 512], P(('grp', 'row')), may hold values from -600 to 600
- counts: int32 [4, 8], P('grp', 'row'), may hold values from 128 to 256, as said below
Outputs:
- new_block: float32 [8192, 512], P(('grp', 'row'))
- factor: float32 [512, 512], replicated
Inputs may be any that keep to these rules, and one draw needn't show every extreme that they name: `counts`: each device's live rows are a multiple of 128, at most 256; one device holds exactly 256.
All inputs are finite; a program needn't handle non-finite values.
Results may differ from a plain program's by a relative error of at most 0.0003.
Values sent between devices are 32-bit elements; how exact they have to be, the bound alone decides.
A program may use at most 64 MiB of HBM per device.

v0:
```python
import jax
import jax.numpy as jnp
from jax import lax
from jax.sharding import PartitionSpec as P


def transposed_product(left, right):
    return lax.dot_general(
        left,
        right,
        (((0,), (0,)), ((), ())),
        precision=lax.Precision.HIGHEST,
        preferred_element_type=jnp.float32,
    )


def matrix_product(left, right):
    return jnp.dot(left, right, precision=lax.Precision.HIGHEST, preferred_element_type=jnp.float32)


def body(basis, block, counts):
    row_slots = block.shape[0]
    devices = lax.axis_size("grp") * lax.axis_size("row")
    weight = 1.0 / (row_slots * devices)
    live = (lax.iota(jnp.int32, row_slots) < counts[0, 0]).astype(jnp.float32)[:, None]
    basis_live = basis * live
    block_live = block * live
    local_coeffs = transposed_product(basis_live, block_live) * weight
    local_metric = transposed_product(basis_live, basis_live) * weight
    coeffs, metric = lax.psum((local_coeffs, local_metric), ("grp", "row"))
    correction = coeffs - matrix_product(metric, coeffs)
    residual = block_live - matrix_product(basis_live, coeffs + correction)
    local_gram = transposed_product(residual, residual) * weight
    gram = lax.psum(local_gram, ("grp", "row"))
    lower_factor = jnp.linalg.cholesky(gram)
    new_block = lax.linalg.triangular_solve(
        lower_factor, residual, left_side=False, lower=True, transpose_a=True
    )
    return (new_block, lower_factor.T)


def solution(mesh):
    placed = (P(("grp", "row"), None), P(("grp", "row"), None), P("grp", "row"))
    return jax.shard_map(
        body, mesh=mesh, in_specs=placed, out_specs=(P(("grp", "row"), None), P()), check_vma=False
    )
```

profile of v0, /device:TPU:0, one launch (start us, length us, event | category | flops | bytes accessed | tf_op | source)
XLA Modules:
  0.0 479.9 jit_solution(1416516150197127453)
XLA Ops:
  7.2 0.0 all-reduce.7.cloned.1.call-start
  7.9 0.0 copy-start
  7.9 0.0 copy-start.4
  7.9 7.3 %convolution_multiply_fusion = f32[1024,1024]{1,0:T(8,128)} fusion(f32[256,1024]{1,0:T(8,128)} %param.3, f32[256]{0:T(256)S(1)} %compare_convert_fusion), kind=kOutput, calls=%fused_computation.3 | convolution fusion | flops 3222536192 | bytes 5243904 | tf_op jit(solution)/shard_map/dot_general | solution.py:8
  15.2 0.0 copy-done
  15.2 0.0 copy-done.4
  15.2 3.3 convolution_multiply_fusion.1
  18.5 0.0 all-reduce.7.cloned.1.call-update
  18.5 0.0 all-reduce.5.cloned.1.call-start
  18.6 159.0 %all-reduce.7.cloned.1.call-done = (f32[1024,512]{1,0:T(8,128)}, f32[1024,1024]{1,0:T(8,128)}) async-done(((f32[1024,512]{1,0:T(8,128)}, f32[1024,1024]{1,0:T(8,128)}), (f32[1024,512]{1,0:T(8,128)}, f32[1024,1024]{1,0:T(8,128)})) %all-reduce.7.cloned.1.call-update) | async-done | bytes 6291472 | tf_op jit(solution)/shard_map/psum | solution.py:30
  177.6 0.0 copy-start.1
  177.6 9.8 %fusion.43 = f32[1024,512]{1,0:T(8,128)S(1)} fusion(f32[1024,1024]{1,0:T(8,128)} %get-tuple-element.21, f32[1024,512]{1,0:T(8,128)} %get-tuple-element.20), kind=kOutput, calls=%fused_computation.84 | convolution fusion | flops 6442450944 | bytes 8388608 | tf_op jit(solution)/shard_map/dot_general | solution.py:18
  187.3 0.0 copy-done.1
  187.3 2.1 fusion.1
  189.5 2.0 convolution_multiply_fusion.2
  191.5 0.0 all-reduce.5.cloned.1.call-update
  191.5 130.7 %all-reduce.5.cloned.1.call-done = f32[512,512]{0,1:T(8,128)} async-done(((f32[512,512]{0,1:T(8,128)}), f32[512,512]{0,1:T(8,128)}) %all-reduce.5.cloned.1.call-update) | async-done | bytes 1048592 | tf_op jit(solution)/shard_map/psum | solution.py:34
  322.2 0.0 copy-start.2
  322.2 1.6 copy.6
  323.9 0.0 copy-done.2
  323.9 0.2 fusion.2
  324.1 0.0 copy-start.3
  324.1 1.0 copy-done.3
  325.1 11.7 %cholesky.104 = f32[128,128]{1,0:T(8,128)S(1)} custom-call(f32[128,128]{1,0:T(8,128)S(1)} %cholesky.266), custom_call_target="Cholesky" | custom-call | tf_op jit(solution)/shard_map/jit(cholesky)/cholesky | solution.py:35
  336.8 9.8 %custom-call.30 = f32[1,128,128]{1,2,0:T(8,128)S(1)} custom-call(f32[1,128,128]{2,1,0:T(8,128)S(1)} %get-tuple-element.35), custom_call_target="InvertDiagBlocksLowerTriangular" | custom-call | tf_op jit(solution)/shard_map/jit(cholesky)/cholesky | solution.py:35
  346.6 0.1 cholesky.224
  346.8 1.2 constant_dynamic-update-slice_fusion.3
  348.0 1.3 convolution_subtract_fusion
  349.3 11.9 %cholesky.217 = f32[128,128]{1,0:T(8,128)S(1)} custom-call(f32[128,128]{1,0:T(8,128)S(1)} %cholesky.270), custom_call_target="Cholesky" | custom-call | tf_op jit(solution)/shard_map/jit(cholesky)/cholesky | solution.py:35
  361.2 9.8 %custom-call.31 = f32[1,128,128]{1,2,0:T(8,128)S(1)} custom-call(f32[1,128,128]{2,1,0:T(8,128)S(1)} %get-tuple-element.32), custom_call_target="InvertDiagBlocksLowerTriangular" | custom-call | tf_op jit(solution)/shard_map/jit(cholesky)/cholesky | solution.py:35
  371.1 0.3 convolution_dynamic-update-slice_fusion
  371.3 1.3 convolution_subtract_fusion.3
  372.6 11.7 %cholesky.238 = f32[128,128]{1,0:T(8,128)S(1)} custom-call(f32[128,128]{1,0:T(8,128)S(1)} %cholesky.275), custom_call_target="Cholesky" | custom-call | tf_op jit(solution)/shard_map/jit(cholesky)/cholesky | solution.py:35
  384.4 0.7 compare_reduce_fusion.1
  385.1 9.8 %custom-call.32 = f32[1,128,128]{1,2,0:T(8,128)S(1)} custom-call(f32[1,128,128]{2,1,0:T(8,128)S(1)} %get-tuple-element.29), custom_call_target="InvertDiagBlocksLowerTriangular" | custom-call | tf_op jit(solution)/shard_map/jit(cholesky)/cholesky | solution.py:35
  394.9 0.2 convolution_dynamic-update-slice_fusion.1
  395.1 1.2 convolution_subtract_fusion.5
  396.4 12.0 %cholesky.255 = f32[128,128]{1,0:T(8,128)S(1)} custom-call(f32[128,128]{1,0:T(8,128)S(1)} %convolution_subtract_fusion.5), custom_call_target="Cholesky" | custom-call | tf_op jit(solution)/shard_map/jit(cholesky)/cholesky | solution.py:35
  408.4 0.6 compare_reduce_fusion
  409.0 0.7 compare_reduce_fusion.2
  412.2 1.2 fusion.7
  413.4 11.7 %while.1 = (s32[]{:T(128)}, f32[512,512]{1,0:T(8,128)}, s32[4,2]{0,1:T(2,128)S(1)}, f32[4,128,128]{2,1,0:T(8,128)S(1)}, s32[]{:T(128)}) while((s32[]{:T(128)}, f32[512,512]{1,0:T(8,128)}, s32[4,2]{0,1:T(2,128)S(1)}, f32[4,128,128]{2,1,0:T(8,128)S(1)}, s32[]{:T(128)}) %tuple.33), condition=%wide.while_cond, body=%wide.while_body.sunk | while | flops 2 | bytes 131181 | solution.py:36
  413.4 0.1 constant_dynamic-slice_fusion.2
  413.5 0.6 fusion.54
  414.1 2.2 bitcast_dynamic-update-slice_fusion.2
  416.4 0.1 constant_dynamic-slice_fusion.2
  416.4 0.6 fusion.54
  417.0 2.2 bitcast_dynamic-update-slice_fusion.2
  419.3 0.1 constant_dynamic-slice_fusion.2
  419.4 0.6 fusion.54
  420.0 2.2 bitcast_dynamic-update-slice_fusion.2
  422.3 0.1 constant_dynamic-slice_fusion.2
  422.3 0.6 fusion.54
  422.9 2.2 bitcast_dynamic-update-slice_fusion.2
  425.1 39.3 %custom-call.33 = f32[4,128,128]{1,2,0:T(8,128)S(1)} custom-call(f32[4,128,128]{2,1,0:T(8,128)S(1)} %get-tuple-element.9), custom_call_target="InvertDiagBlocksLowerTriangular" | custom-call | tf_op jit(solution)/shard_map/triangular_solve | solution.py:36
  464.5 0.3 fusion.29
  464.8 1.2 convolution_subtract_fusion.4
  466.0 0.3 fusion.33
  466.3 1.5 convolution_subtract_fusion.2
  467.8 0.3 fusion.32
  468.2 1.8 convolution_subtract_fusion.1
  469.9 0.3 fusion.31
  470.3 1.0 copy.7
  471.3 1.3 copy.8
  (12 shorter events, 0.2 us)
Async XLA Ops:
  7.2 170.4 %all-reduce.7.cloned.1.call-start = ((), (), s32[]{:S(2)}) async-start(), calls=%async_computation.1 | async-start | bytes 12582912 | tf_op jit(solution)/shard_map/psum | solution.py:30
  7.9 7.4 %copy-start = (f32[256,1024]{1,0:T(8,128)S(1)}, f32[256,1024]{1,0:T(8,128)}, u32[]{:S(2)}) copy-start(f32[256,1024]{1,0:T(8,128)} %param.3) | copy-start | bytes 3145732
  7.9 7.3 %copy-start.4 = (f32[256,512]{1,0:T(8,128)S(1)}, f32[256,512]{1,0:T(8,128)}, u32[]{:S(2)}) copy-start(f32[256,512]{1,0:T(8,128)} %param.4) | copy-start | bytes 1572868
  18.5 303.7 %all-reduce.5.cloned.1.call-start = ((), (), s32[]{:S(2)}) async-start(), calls=%async_computation | async-start | bytes 2097152 | tf_op jit(solution)/shard_map/psum | solution.py:34
  177.6 9.8 %copy-start.1 = (f32[1024,512]{1,0:T(8,128)S(1)}, f32[1024,512]{1,0:T(8,128)}, u32[]{:S(2)}) copy-start(f32[1024,512]{1,0:T(8,128)} %get-tuple-element.20) | copy-start | bytes 6291460
  322.2 1.7 copy-start.2
  324.1 1.0 copy-start.3
Sparse Core Ops, SparseCore 0:
  18.7 158.8 all-reduce.6
  191.6 130.5 all-reduce.4
where the time goes:
time: 487 us; the launch traced here: 480 us
  waiting for transfers between devices  290 us (60%)
  other arithmetic  120 us (25%)
  matrix products  35.7 us (7%)
  between operations  17.9 us (4%)
  local copies, waits for them, and re-layouts  16.7 us (3%)
    psum x1, waiting for transfers between devices, body(): coeffs, metric = lax.psum((local_coeffs, local_metric), ('grp', 'row'))  159 us
    psum x1, waiting for transfers between devices, body(): gram = lax.psum(local_gram, ('grp', 'row'))  131 us
    another operation x14, other arithmetic, body(): lower_factor = jnp.linalg.cholesky(gram)  78.9 us
    another operation x3, other arithmetic, body(): lax.linalg.triangular_solve(lower_factor, residual, left_side=False, lowe...  39.4 us
    dot_general x3, matrix products, transposed_product(): lax.dot_general(left, right, (((0,), (0,)), ((), ())), precision=lax.Prec...  12.6 us
    dot_general x2, matrix products, matrix_product(): jnp.dot(left, right, precision=lax.Precision.HIGHEST, preferred_element_t...  11.9 us
    another operation x12, local copies, waits for them, and re-layouts  11.6 us
  transfers between devices with their start and end apart: 2, of which 2 were waited for; matrix products, arithmetic and copies ran while one was open for 0% of the time, Pallas kernels for 0%

commit v1 on v0

v1 whole, which is shorter than its diff:
```python
import functools

import jax
import jax.numpy as jnp
from jax import lax
from jax.experimental import pallas as pl
from jax.experimental.pallas import tpu as pltpu
from jax.sharding import PartitionSpec as P

HIGHEST = lax.Precision.HIGHEST
MESH = pl.DeviceIdType.MESH
TILE = 128


def transposed_product(left, right):
    return lax.dot_general(
        left,
        right,
        (((0,), (0,)), ((), ())),
        precision=HIGHEST,
        preferred_element_type=jnp.float32,
    )


def matrix_product(left, right):
    return jnp.dot(left, right, precision=HIGHEST, preferred_element_type=jnp.float32)


def column_split(rows, cols, first, second):
    split = 1
    while split <= second and cols % (split * TILE) == 0:
        if rows % first == 0 and (rows // first) % (second // split * 8) == 0:
            return split
        split *= 2
    return None


def plan_parts(rows, cols, sizes):
    half = cols // 2
    parts = []
    for start, order in ((0, ("row", "grp")), (half, ("grp", "row"))):
        parts.append((start, half, order, column_split(rows, half, sizes[order[0]], sizes[order[1]])))
    if all(part[3] is not None for part in parts):
        return parts
    order = ("row", "grp")
    split = column_split(rows, cols, sizes["row"], sizes["grp"])
    assert split is not None
    return [(0, cols, order, split)]


def all_reduce_kernel(parts, sizes, x_ref, out_ref, *scratch):
    rows = x_ref.shape[0]
    me = {axis: lax.axis_index(axis) for axis in sizes}

    def ahead(axis, k):
        return lax.rem(me[axis] + k, sizes[axis])

    barrier = pltpu.get_barrier_semaphore()
    for axis in sizes:
        for k in range(1, sizes[axis]):
            pl.semaphore_signal(barrier, inc=1, device_id={axis: ahead(axis, k)}, device_id_type=MESH)
    pl.semaphore_wait(barrier, sum(size - 1 for size in sizes.values()))

    groups = [scratch[7 * i : 7 * i + 7] for i in range(len(parts))]

    def first_chunk(part, index):
        start, width, order, _ = part
        height = rows // sizes[order[0]]
        return pl.ds(pl.multiple_of(index * height, 8), height), pl.ds(start, width)

    def second_chunk(part, index):
        start, width, order, split = part
        height = rows // sizes[order[0]] // (sizes[order[1]] // split)
        piece = width // split
        if split == 1:
            return pl.multiple_of(index * height, 8), height, start, 0, piece
        row = pl.multiple_of(lax.div(index, split) * height, 8)
        offset = pl.multiple_of(lax.rem(index, split) * piece, TILE)
        return row, height, start + offset, offset, piece

    def send(source, target, send_sem, recv_sem, axis, k):
        copy = pltpu.make_async_remote_copy(
            src_ref=source,
            dst_ref=target,
            send_sem=send_sem,
            recv_sem=recv_sem,
            device_id={axis: ahead(axis, k)},
            device_id_type=MESH,
        )
        copy.start()
        return copy

    sent = []
    stage = [[] for _ in parts]
    most = max(sizes.values())
    for k in range(1, most):
        for i, part in enumerate(parts):
            axis = part[2][0]
            if k < sizes[axis]:
                held, _, _, sends, recvs, _, _ = groups[i]
                rs, cs = first_chunk(part, ahead(axis, k))
                stage[i].append(
                    send(x_ref.at[rs, cs], held.at[k - 1], sends.at[k - 1], recvs.at[k - 1], axis, k)
                )
    for i, part in enumerate(parts):
        axis, other = part[2]
        held, partial, held_second, _, _, sends, recvs = groups[i]
        for copy in stage[i]:
            copy.wait_recv()
        rs, cs = first_chunk(part, me[axis])
        total = x_ref[rs, cs]
        for k in range(sizes[axis] - 1):
            total = total + held[k]
        partial[...] = total
        sent += stage[i]
        stage[i] = []
        for k in range(1, sizes[other]):
            row, height, _, offset, piece = second_chunk(part, ahead(other, k))
            stage[i].append(
                send(
                    partial.at[pl.ds(row, height), pl.ds(offset, piece)],
                    held_second.at[k - 1],
                    sends.at[0, k - 1],
                    recvs.at[0, k - 1],
                    other,
                    k,
                )
            )
    for i, part in enumerate(parts):
        axis, other = part[2]
        _, partial, held_second, _, _, sends, recvs = groups[i]
        for copy in stage[i]:
            copy.wait_recv()
        row, height, column, offset, piece = second_chunk(part, me[other])
        total = partial[pl.ds(row, height), pl.ds(offset, piece)]
        for k in range(sizes[other] - 1):
            total = total + held_second[k]
        base = me[axis] * (rows // sizes[axis])
        place = out_ref.at[pl.ds(pl.multiple_of(base + row, 8), height), pl.ds(column, piece)]
        place[...] = total
        sent += stage[i]
        stage[i] = []
        for k in range(1, sizes[other]):
            stage[i].append(send(place, place, sends.at[1, k - 1], recvs.at[1, k - 1], other, k))
    for i, part in enumerate(parts):
        axis, _ = part[2]
        final_sends, final_recvs = scratch[7 * len(parts) + 2 * i : 7 * len(parts) + 2 * i + 2]
        for copy in stage[i]:
            copy.wait_recv()
        sent += stage[i]
        stage[i] = []
        rs, cs = first_chunk(part, me[axis])
        place = out_ref.at[rs, cs]
        for k in range(1, sizes[axis]):
            stage[i].append(send(place, place, final_sends.at[k - 1], final_recvs.at[k - 1], axis, k))
    for i in range(len(parts)):
        for copy in stage[i]:
            copy.wait_recv()
        sent += stage[i]
    for copy in sent:
        copy.wait_send()


def all_reduce(x, collective_id):
    rows, cols = x.shape
    sizes = {axis: lax.axis_size(axis) for axis in ("grp", "row")}
    parts = plan_parts(rows, cols, sizes)
    scratch = []
    for _, width, (axis, other), split in parts:
        height = rows // sizes[axis]
        scratch += [
            pltpu.VMEM((sizes[axis] - 1, height, width), jnp.float32),
            pltpu.VMEM((height, width), jnp.float32),
            pltpu.VMEM((sizes[other] - 1, height // (sizes[other] // split), width // split), jnp.float32),
            pltpu.SemaphoreType.DMA((sizes[axis] - 1,)),
            pltpu.SemaphoreType.DMA((sizes[axis] - 1,)),
            pltpu.SemaphoreType.DMA((2, sizes[other] - 1)),
            pltpu.SemaphoreType.DMA((2, sizes[other] - 1)),
        ]
    for _, _, (axis, _), _ in parts:
        scratch += [pltpu.SemaphoreType.DMA((sizes[axis] - 1,))] * 2
    return pl.pallas_call(
        functools.partial(all_reduce_kernel, parts, sizes),
        out_shape=jax.ShapeDtypeStruct((rows, cols), jnp.float32),
        in_specs=[pl.BlockSpec(memory_space=pltpu.VMEM)],
        out_specs=pl.BlockSpec(memory_space=pltpu.VMEM),
        scratch_shapes=scratch,
        compiler_params=pltpu.CompilerParams(collective_id=collective_id, has_side_effects=True),
        name=f"all_reduce_{collective_id}",
    )(x)


def eliminate(block):
    size = block.shape[0]
    count = size // 8
    sub = lax.broadcasted_iota(jnp.int32, (8, size), 0)
    lane = lax.broadcasted_iota(jnp.int32, (8, size), 1)
    left = [block[8 * b : 8 * b + 8] for b in range(count)]
    right = [(lane == sub + 8 * b).astype(jnp.float32) for b in range(count)]
    for j in range(size):
        home, inner = divmod(j, 8)
        row = left[home][inner : inner + 1]
        companion = right[home][inner : inner + 1]
        inverse = 1.0 / row[:, j : j + 1]
        row = row * inverse
        companion = companion * inverse
        for b in range(home, count):
            if b == home and inner == 7:
                continue
            factor = jnp.broadcast_to(left[b][:, j : j + 1], (8, size))
            if b == home:
                factor = jnp.where(sub > inner, factor, 0.0)
            left[b] = left[b] - factor * row
            right[b] = right[b] - factor * companion
    upper, inverted = [], []
    for b in range(count):
        diagonal = jnp.sum(jnp.where(lane == sub + 8 * b, left[b], 0.0), axis=1, keepdims=True)
        root = 1.0 / jnp.sqrt(diagonal)
        upper.append(jnp.where(lane >= sub + 8 * b, left[b] * root, 0.0))
        inverted.append(jnp.where(lane <= sub + 8 * b, right[b] * root, 0.0))
    return jnp.concatenate(upper, axis=0), jnp.concatenate(inverted, axis=0)


def factor_kernel(gram_ref, residual_ref, new_ref, factor_ref, work, rest):
    size = gram_ref.shape[0]
    work[...] = gram_ref[...]
    rest[...] = residual_ref[...]

    def step(index, carry):
        window = pl.ds(pl.multiple_of(index * TILE, TILE), TILE)
        upper, inverted = eliminate(work[window, window])
        panel = matrix_product(inverted, work[window, :])
        column = lax.broadcasted_iota(jnp.int32, (TILE, size), 1)
        panel = jnp.where(column >= (index + 1) * TILE, panel, 0.0)
        factor_ref[window, :] = panel
        factor_ref[window, window] = upper
        work[...] -= transposed_product(panel, panel)
        solved = lax.dot_general(
            rest[:, window],
            inverted,
            (((1,), (1,)), ((), ())),
            precision=HIGHEST,
            preferred_element_type=jnp.float32,
        )
        new_ref[:, window] = solved
        rest[...] -= matrix_product(solved, panel)
        return carry

    lax.fori_loop(0, size // TILE, step, 0)


def factor_and_solve(gram, residual):
    vmem = pl.BlockSpec(memory_space=pltpu.VMEM)
    return pl.pallas_call(
        factor_kernel,
        out_shape=(
            jax.ShapeDtypeStruct(residual.shape, jnp.float32),
            jax.ShapeDtypeStruct(gram.shape, jnp.float32),
        ),
        in_specs=[vmem, vmem],
        out_specs=(vmem, vmem),
        scratch_shapes=[pltpu.VMEM(gram.shape, jnp.float32), pltpu.VMEM(residual.shape, jnp.float32)],
        name="factor_and_solve",
    )(gram, residual)


def body(basis, block, counts):
    row_slots = block.shape[0]
    devices = lax.axis_size("grp") * lax.axis_size("row")
    weight = 1.0 / (row_slots * devices)
    live = (lax.iota(jnp.int32, row_slots) < counts[0, 0]).astype(jnp.float32)[:, None]
    basis_live = basis * live
    block_live = block * live
    coeffs = all_reduce(transposed_product(basis_live, block_live) * weight, 0)
    first_pass = block_live - matrix_product(basis_live, coeffs)
    correction = all_reduce(transposed_product(basis_live, first_pass) * weight, 1)
    residual = first_pass - matrix_product(basis_live, correction)
    gram = all_reduce(transposed_product(residual, residual) * weight, 2)
    return factor_and_solve(gram, residual)


def solution(mesh):
    placed = (P(("grp", "row"), None), P(("grp", "row"), None), P("grp", "row"))
    return jax.shard_map(
        body, mesh=mesh, in_specs=placed, out_specs=(P(("grp", "row"), None), P()), check_vma=False
    )
```

time: 487 us -> 242 us (0.50)
  waiting for transfers between devices: 290 us -> 0 us
  Pallas kernels: 0 us -> 221 us
  other arithmetic: 120 us -> 0.01 us
  matrix products: 35.7 us -> 17.1 us
  local copies, waits for them, and re-layouts: 16.7 us -> 0.01 us
  between operations: 17.9 us -> 1.36 us
    psum x2 -> x0, waiting for transfers between devices: 290 us -> none  [the longest x1 159 us: body(): coeffs, metric = lax.psum((local_coeffs, local_metric), ('grp', 'row'))]
    pallas_call x0 -> x4, Pallas kernels: none -> 221 us  [the longest x3 168 us: all_reduce(): pl.pallas_call(functools.partial(all_reduce_kernel, parts, sizes), out_sh...]
    another operation x17 -> x0, other arithmetic: 118 us -> none  [the longest x14 78.9 us: body(): lower_factor = jnp.linalg.cholesky(gram)]
    another operation x17 -> x0, local copies, waits for them, and re-layouts: 11.8 us -> none
    another operation x13 -> x0, matrix products: 11.2 us -> none  [the longest x7 5.74 us: body(): lax.linalg.triangular_solve(lower_factor, residual, left_side=False, lowe...]
    dot_general x5, matrix products: 24.5 us -> 17.1 us  [the longest x3 9.96 us: transposed_product(): lax.dot_general(left, right, (((0,), (0,)), ((), ())), precision=HIGHEST,...]
  transfers between devices with their start and end apart: 2 -> 0, of which waited for: 2 -> 0; matrix products, arithmetic and copies ran while one was open for 0% -> 0% of each run, Pallas kernels for 0% -> 0%
where the time goes in v1:
time: 242 us; the launch traced here: 239 us
  Pallas kernels  221 us (91%)
  matrix products  17.1 us (7%)
    pallas_call x3, Pallas kernels, all_reduce(): pl.pallas_call(functools.partial(all_reduce_kernel, parts, sizes), out_sh...  168 us
    pallas_call x1, Pallas kernels, factor_and_solve(): pl.pallas_call(factor_kernel, out_shape=(jax.ShapeDtypeStruct(residual.sh...  52.8 us
    dot_general x3, matrix products, transposed_product(): lax.dot_general(left, right, (((0,), (0,)), ((), ())), precision=HIGHEST,...  9.96 us
    dot_general x2, matrix products, matrix_product(): jnp.dot(left, right, precision=HIGHEST, preferred_element_type=jnp.float32)  7.12 us

profile of v1, /device:TPU:0, one launch (start us, length us, event | category | flops | bytes accessed | tf_op | source)
XLA Modules:
  0.0 239.3 jit_solution(9111786552993633946)
XLA Ops:
  1.3 4.7 %convolution_multiply_fusion.1.x_ref = f32[1024,512]{1,0:T(8,128)} fusion(f32[256,1024]{1,0:T(8,128)} %param.3, f32[256]{0:T(256)S(1)} %compare_convert_fusion, f32[256,512]{1,0:T(8,128)} %param.4), kind=kOutput, calls=%fused_computation.1 | convolution fusion | flops 1611530240 | bytes 3671040 | tf_op jit(solution)/shard_map/dot_general | solution.py:16
  6.0 0.0 copy-start
  6.0 0.0 copy-start.2
  6.0 58.7 %all_reduce_0.1 = f32[1024,512]{1,0:T(8,128)} custom-call(f32[1024,512]{1,0:T(8,128)} %convolution_multiply_fusion.1.x_ref), custom_call_target="tpu_custom_call" | custom-call | tf_op jit(solution)/shard_map/all_reduce_0/pallas_call | solution.py:182
  64.7 0.0 copy-done
  64.7 0.0 copy-done.2
  64.7 3.6 %convolution_subtract_fusion.1 = f32[256,512]{1,0:T(8,128)S(1)} fusion(f32[1024,512]{1,0:T(8,128)} %all_reduce_0.1, f32[256,1024]{1,0:T(8,128)S(1)} %copy-done, f32[256]{0:T(256)S(1)} %compare_convert_fusion, f32[256,512]{1,0:T(8,128)S(1)} %copy-done.2), kind=kOutput, calls=%fused_computation.4 | convolution fusion | flops 1611137024 | bytes 4195328 | tf_op jit(solution)/shard_map/dot_general | solution.py:26
  68.3 3.3 %convolution_multiply_fusion.x_ref = f32[1024,512]{1,0:T(8,128)} fusion(f32[256,512]{1,0:T(8,128)S(1)} %convolution_subtract_fusion.1, f32[256,1024]{1,0:T(8,128)S(1)} %copy-done, f32[256]{0:T(256)S(1)} %compare_convert_fusion), kind=kOutput, calls=%fused_computation | convolution fusion | flops 1611399168 | bytes 3671040 | tf_op jit(solution)/shard_map/dot_general | solution.py:16
  71.6 66.5 %all_reduce_1.1 = f32[1024,512]{1,0:T(8,128)} custom-call(f32[1024,512]{1,0:T(8,128)} %convolution_multiply_fusion.x_ref), custom_call_target="tpu_custom_call" | custom-call | tf_op jit(solution)/shard_map/all_reduce_1/pallas_call | solution.py:182
  138.1 3.6 %convolution_subtract_fusion.residual_ref = f32[256,512]{1,0:T(8,128)S(1)} fusion(f32[256,512]{1,0:T(8,128)S(1)} %convolution_subtract_fusion.1, f32[1024,512]{1,0:T(8,128)} %all_reduce_1.1, f32[256,1024]{1,0:T(8,128)S(1)} %copy-done, f32[256]{0:T(256)S(1)} %compare_convert_fusion), kind=kOutput, calls=%fused_computation.3 | convolution fusion | flops 1611005952 | bytes 4195328 | tf_op jit(solution)/shard_map/dot_general | solution.py:26
  141.7 0.0 copy-start.1
  141.7 2.0 convolution_multiply_fusion.2.x_ref
  143.7 42.9 %all_reduce_2.1.gram_ref = f32[512,512]{1,0:T(8,128)} custom-call(f32[512,512]{1,0:T(8,128)} %convolution_multiply_fusion.2.x_ref), custom_call_target="tpu_custom_call" | custom-call | tf_op jit(solution)/shard_map/all_reduce_2/pallas_call | solution.py:182
  186.6 0.0 copy-done.1
  186.6 52.8 %factor_and_solve.1 = (f32[256,512]{1,0:T(8,128)}, f32[512,512]{1,0:T(8,128)}) custom-call(f32[512,512]{1,0:T(8,128)} %all_reduce_2.1.gram_ref, f32[256,512]{1,0:T(8,128)} %copy-done.1), custom_call_target="tpu_custom_call" | custom-call | tf_op jit(solution)/shard_map/factor_and_solve/pallas_call | solution.py:254
  (1 shorter events, 0.0 us)
Async XLA Ops:
  6.0 58.7 %copy-start = (f32[256,1024]{1,0:T(8,128)S(1)}, f32[256,1024]{1,0:T(8,128)}, u32[]{:S(2)}) copy-start(f32[256,1024]{1,0:T(8,128)} %param.3) | copy-start | bytes 3145732
  6.0 58.7 %copy-start.2 = (f32[256,512]{1,0:T(8,128)S(1)}, f32[256,512]{1,0:T(8,128)}, u32[]{:S(2)}) copy-start(f32[256,512]{1,0:T(8,128)} %param.4) | copy-start | bytes 1572868
  141.7 44.9 %copy-start.1 = (f32[256,512]{1,0:T(8,128)}, f32[256,512]{1,0:T(8,128)S(1)}, u32[]{:S(2)}) copy-start(f32[256,512]{1,0:T(8,128)S(1)} %convolution_subtract_fusion.residual_ref) | copy-start | bytes 1572868

commit v2 on v1

--- a/solution.py
+++ b/solution.py
@@ -197,21 +197,26 @@
     lane = lax.broadcasted_iota(jnp.int32, (8, size), 1)
     left = [block[8 * b : 8 * b + 8] for b in range(count)]
     right = [(lane == sub + 8 * b).astype(jnp.float32) for b in range(count)]
-    for j in range(size):
+    for j in range(0, size, 2):
         home, inner = divmod(j, 8)
-        row = left[home][inner : inner + 1]
-        companion = right[home][inner : inner + 1]
+        row, next_row = left[home][inner : inner + 1], left[home][inner + 1 : inner + 2]
+        mate, next_mate = right[home][inner : inner + 1], right[home][inner + 1 : inner + 2]
         inverse = 1.0 / row[:, j : j + 1]
+        ratio = row[:, j + 1 : j + 2] * inverse
+        pivot = next_row[:, j + 1 : j + 2] - ratio * row[:, j + 1 : j + 2]
+        next_inverse = 1.0 / pivot
+        next_row = (next_row - ratio * row) * next_inverse
+        next_mate = (next_mate - ratio * mate) * next_inverse
         row = row * inverse
-        companion = companion * inverse
+        mate = mate * inverse
         for b in range(home, count):
-            if b == home and inner == 7:
-                continue
             factor = jnp.broadcast_to(left[b][:, j : j + 1], (8, size))
+            next_factor = jnp.broadcast_to(left[b][:, j + 1 : j + 2], (8, size)) - factor * ratio
             if b == home:
                 factor = jnp.where(sub > inner, factor, 0.0)
-            left[b] = left[b] - factor * row
-            right[b] = right[b] - factor * companion
+                next_factor = jnp.where(sub > inner + 1, next_factor, 0.0)
+            left[b] = left[b] - factor * row - next_factor * next_row
+            right[b] = right[b] - factor * mate - next_factor * next_mate
     upper, inverted = [], []
     for b in range(count):
         diagonal = jnp.sum(jnp.where(lane == sub + 8 * b, left[b], 0.0), axis=1, keepdims=True)

time: 242 us -> 250 us (1.033)
  Pallas kernels: 221 us -> 229 us
    pallas_call x1, Pallas kernels: 52.8 us -> 61 us  [factor_and_solve(): pl.pallas_call(factor_kernel, out_shape=(jax.ShapeDtypeStruct(residual.sh...]
where the time goes in v2:
time: 250 us; the launch traced here: 248 us
  Pallas kernels  229 us (92%)
  matrix products  17.1 us (7%)
    pallas_call x3, Pallas kernels, all_reduce(): pl.pallas_call(functools.partial(all_reduce_kernel, parts, sizes), out_sh...  168 us
    pallas_call x1, Pallas kernels, factor_and_solve(): pl.pallas_call(factor_kernel, out_shape=(jax.ShapeDtypeStruct(residual.sh...  61 us
    dot_general x3, matrix products, transposed_product(): lax.dot_general(left, right, (((0,), (0,)), ((), ())), precision=HIGHEST,...  9.96 us
    dot_general x2, matrix products, matrix_product(): jnp.dot(left, right, precision=HIGHEST, preferred_element_type=jnp.float32)  7.12 us

profile of v2, /device:TPU:0, one launch (start us, length us, event | category | flops | bytes accessed | tf_op | source)
XLA Modules:
  0.0 247.5 jit_solution(9154407747960354228)
XLA Ops:
  1.3 4.7 %convolution_multiply_fusion.1.x_ref = f32[1024,512]{1,0:T(8,128)} fusion(f32[256,1024]{1,0:T(8,128)} %param.3, f32[256]{0:T(256)S(1)} %compare_convert_fusion, f32[256,512]{1,0:T(8,128)} %param.4), kind=kOutput, calls=%fused_computation.1 | convolution fusion | flops 1611530240 | bytes 3671040 | tf_op jit(solution)/shard_map/dot_general | solution.py:16
  6.0 0.0 copy-start
  6.0 0.0 copy-start.2
  6.0 58.7 %all_reduce_0.1 = f32[1024,512]{1,0:T(8,128)} custom-call(f32[1024,512]{1,0:T(8,128)} %convolution_multiply_fusion.1.x_ref), custom_call_target="tpu_custom_call" | custom-call | tf_op jit(solution)/shard_map/all_reduce_0/pallas_call | solution.py:182
  64.7 0.0 copy-done
  64.7 0.0 copy-done.2
  64.7 3.6 %convolution_subtract_fusion.1 = f32[256,512]{1,0:T(8,128)S(1)} fusion(f32[1024,512]{1,0:T(8,128)} %all_reduce_0.1, f32[256,1024]{1,0:T(8,128)S(1)} %copy-done, f32[256]{0:T(256)S(1)} %compare_convert_fusion, f32[256,512]{1,0:T(8,128)S(1)} %copy-done.2), kind=kOutput, calls=%fused_computation.4 | convolution fusion | flops 1611137024 | bytes 4195328 | tf_op jit(solution)/shard_map/dot_general | solution.py:26
  68.3 3.3 %convolution_multiply_fusion.x_ref = f32[1024,512]{1,0:T(8,128)} fusion(f32[256,512]{1,0:T(8,128)S(1)} %convolution_subtract_fusion.1, f32[256,1024]{1,0:T(8,128)S(1)} %copy-done, f32[256]{0:T(256)S(1)} %compare_convert_fusion), kind=kOutput, calls=%fused_computation | convolution fusion | flops 1611399168 | bytes 3671040 | tf_op jit(solution)/shard_map/dot_general | solution.py:16
  71.6 66.5 %all_reduce_1.1 = f32[1024,512]{1,0:T(8,128)} custom-call(f32[1024,512]{1,0:T(8,128)} %convolution_multiply_fusion.x_ref), custom_call_target="tpu_custom_call" | custom-call | tf_op jit(solution)/shard_map/all_reduce_1/pallas_call | solution.py:182
  138.1 3.6 %convolution_subtract_fusion.residual_ref = f32[256,512]{1,0:T(8,128)S(1)} fusion(f32[256,512]{1,0:T(8,128)S(1)} %convolution_subtract_fusion.1, f32[1024,512]{1,0:T(8,128)} %all_reduce_1.1, f32[256,1024]{1,0:T(8,128)S(1)} %copy-done, f32[256]{0:T(256)S(1)} %compare_convert_fusion), kind=kOutput, calls=%fused_computation.3 | convolution fusion | flops 1611005952 | bytes 4195328 | tf_op jit(solution)/shard_map/dot_general | solution.py:26
  141.7 0.0 copy-start.1
  141.7 2.0 convolution_multiply_fusion.2.x_ref
  143.7 42.9 %all_reduce_2.1.gram_ref = f32[512,512]{1,0:T(8,128)} custom-call(f32[512,512]{1,0:T(8,128)} %convolution_multiply_fusion.2.x_ref), custom_call_target="tpu_custom_call" | custom-call | tf_op jit(solution)/shard_map/all_reduce_2/pallas_call | solution.py:182
  186.6 0.0 copy-done.1
  186.6 61.0 %factor_and_solve.1 = (f32[256,512]{1,0:T(8,128)}, f32[512,512]{1,0:T(8,128)}) custom-call(f32[512,512]{1,0:T(8,128)} %all_reduce_2.1.gram_ref, f32[256,512]{1,0:T(8,128)} %copy-done.1), custom_call_target="tpu_custom_call" | custom-call | tf_op jit(solution)/shard_map/factor_and_solve/pallas_call | solution.py:259
  (1 shorter events, 0.0 us)
Async XLA Ops:
  6.0 58.7 %copy-start = (f32[256,1024]{1,0:T(8,128)S(1)}, f32[256,1024]{1,0:T(8,128)}, u32[]{:S(2)}) copy-start(f32[256,1024]{1,0:T(8,128)} %param.3) | copy-start | bytes 3145732
  6.0 58.7 %copy-start.2 = (f32[256,512]{1,0:T(8,128)S(1)}, f32[256,512]{1,0:T(8,128)}, u32[]{:S(2)}) copy-start(f32[256,512]{1,0:T(8,128)} %param.4) | copy-start | bytes 1572868
  141.7 44.9 %copy-start.1 = (f32[256,512]{1,0:T(8,128)}, f32[256,512]{1,0:T(8,128)S(1)}, u32[]{:S(2)}) copy-start(f32[256,512]{1,0:T(8,128)S(1)} %convolution_subtract_fusion.residual_ref) | copy-start | bytes 1572868
